TPU v7x, 32 devices: a whole 2x2x4 slice. The times are simulated.
32 devices in a mesh: row: 4 (over z), mix: 8 (over y, x, core).
Axes of the slice: x: 2, y: 2, z: 4, core: 2. Of those that a mesh axis runs over, the one named last changes fastest.
Arguments:
- velocity: bfloat16 [64, 3, 8, 32, 128], P(None, None, 'mix', 'row'), may hold values from -6 to 6
- field_b: bfloat16 [64, 3, 8, 32, 128], P(None, None, 'mix', 'row'), may hold values from -6 to 6
- test_signs: int32 [384, 256], replicated, may hold values from 0 to 1
- row_signs: int32 [8, 32, 128], P('mix', 'row'), may hold values from 0 to 1
- sample_index: int32 [8, 4, 256], P('mix', 'row'), may hold values from 0 to 1023
Outputs:
- basis_rows: float32 [8, 4, 256, 256], P('mix', 'row')
- factor: float32 [256, 256], replicated
Inputs may be any that keep to these rules, and one draw needn't show every extreme that they name: test_signs entries are bits; the test matrix is 2 test_signs - 1. row_signs entries are bits; the sign is 2 row_signs - 1. `sample_index`: a point of the device's own block, p = x_local 128 + y; repeats may occur.
All inputs are finite; a program needn't handle non-finite values.
Results may differ from a plain program's by a relative error of at most 0.0021.
Values may be sent and summed in bfloat16 or wider, within the bound.
No kernel may reach another device: no remote copies, remote signals or barrier semaphores. Data moves between devices by JAX's collectives and lax.ppermute only.
A program may use at most 64 MiB of HBM per device.

v0:
```python
import math
import jax
import jax.numpy as jnp
from jax import lax
from jax.sharding import PartitionSpec as P


def swapped(block, axis, distance):
    count = lax.axis_size(axis)
    route = []
    for low in range(count):
        high = low | 1 << distance
        if high != low and high < count:
            route += [(low, high), (high, low)]
    return lax.ppermute(block, axis, route)


def padded(shard, sides, width):
    for axis, dim in sides:
        size, length = (lax.axis_size(axis), shard.shape[dim])
        up = [(i, (i + 1) % size) for i in range(size - 1)]
        down = [(j, i) for i, j in up]
        last = lax.slice_in_dim(shard, length - width, length, axis=dim)
        first = lax.slice_in_dim(shard, 0, width, axis=dim)
        before = lax.ppermute(last, axis, up)
        after = lax.ppermute(first, axis, down)
        shard = jnp.concatenate([before, shard, after], axis=dim)
    return shard


def curl_plane(stencil_slab):
    center = stencil_slab[:, :, 1]

    def along_x(component):
        return (center[:, component, 2:, 1:-1] - center[:, component, :-2, 1:-1]) * 0.5

    def along_y(component):
        return (center[:, component, 1:-1, 2:] - center[:, component, 1:-1, :-2]) * 0.5

    def along_z(component):
        return (
            stencil_slab[:, component, 2, 1:-1, 1:-1] - stencil_slab[:, component, 0, 1:-1, 1:-1]
        ) * 0.5

    current_x = along_y(2) - along_z(1)
    current_y = along_z(0) - along_x(2)
    current_z = along_x(1) - along_y(0)
    return jnp.stack([current_x, current_y, current_z], axis=1).astype(jnp.bfloat16)


def pair_mixing(signed, planes):
    my_index = lax.axis_index("mix")
    values = signed
    for level in range(planes.bit_length() - 1):
        partner = swapped(values, "mix", level)
        upper_bit = my_index // (1 << level) % 2
        values = jnp.where(upper_bit == 1, partner - values, values + partner)
    return values / math.sqrt(planes)


def upper_factor(gram_matrix):
    return jnp.linalg.cholesky(gram_matrix).T


def on_device(velocity, field_b, test_signs, row_signs, sample_index):
    snaps = field_b.shape[0]
    sketch_width = test_signs.shape[1]
    planes = lax.axis_size("mix")
    row_blocks = lax.axis_size("row")
    with_rims = padded(field_b, (("row", 3), ("mix", 2)), 1)
    stencil_slab = jnp.pad(with_rims.astype(jnp.float32), ((0, 0), (0, 0), (0, 0), (0, 0), (1, 1)))
    current = curl_plane(stencil_slab)
    snapshot = jnp.concatenate([velocity[:, :, 0], current], axis=1).reshape(6 * snaps, -1)
    test_matrix = (2 * test_signs - 1).astype(jnp.bfloat16)
    sketch = lax.dot_general(
        snapshot, test_matrix, (((0,), (0,)), ((), ())), preferred_element_type=jnp.float32
    ) * (1.0 / math.sqrt(6 * snaps))
    point_signs = (2 * row_signs - 1).astype(jnp.float32).reshape(-1)
    signed = sketch * point_signs[:, None]
    mixed_rows = pair_mixing(signed, planes)
    picked = jnp.take(mixed_rows, sample_index.reshape(-1), axis=0)
    picked_total = planes * row_blocks * picked.shape[0]
    local_gram = (
        jnp.dot(
            picked.T, picked, precision=lax.Precision.HIGHEST, preferred_element_type=jnp.float32
        )
        / picked_total
    )
    block_factor = upper_factor(lax.psum(local_gram, "mix"))
    every_factor = lax.all_gather(block_factor[None], "row", axis=0, tiled=True)
    stacked_gram = jnp.einsum(
        "bij,bil->jl", every_factor, every_factor, precision=lax.Precision.HIGHEST
    )
    factor = upper_factor(stacked_gram)
    solved = jax.scipy.linalg.solve_triangular(factor.T, picked.T, lower=True)
    basis_rows = solved.T.reshape(sample_index.shape + (sketch_width,))
    return (basis_rows, factor)


def solution(mesh):
    return jax.shard_map(
        on_device,
        mesh=mesh,
        in_specs=(
            P(None, None, "mix", "row", None),
            P(None, None, "mix", "row", None),
            P(),
            P("mix", "row", None),
            P("mix", "row", None),
        ),
        out_specs=(P("mix", "row", None, None), P()),
        check_vma=False,
    )
```

profile of v0, /device:TPU:0, one launch (start us, length us, event | category | flops | bytes accessed | tf_op | source)
XLA Modules:
  0.0 284.6 jit_solution(11077461579640509562)
XLA Ops:
  7.2 1.4 fusion.46
  8.6 4.9 %collective-permute-start = (bf16[64,3,1,1,128]{4,0,3,2,1:T(8,128)(2,1)S(1)}, bf16[64,3,1,1,128]{4,0,3,2,1:T(8,128)(2,1)S(1)}, u32[]{:S(2)}, u32[]{:S(2)}) collective-permute-start(bf16[64,3,1,1,128]{4,0,3,2,1:T(8,128)(2,1)S(1)} %copy.62), channel_id=1, source_target_pairs={{0,8},{8,16},{16,24},{1,9},{9,17},{17,25},{2,10},{10,18},{18,26},{... | collective-permute-start | bytes 147464 | tf_op jit(solution)/shard_map/ppermute | solution.py:25
  13.6 1.3 collective-permute-start.1
  15.3 1.1 constant_dynamic-update-slice_fusion.1
  16.4 3.2 %collective-permute-done.1 = bf16[64,3,1,1,128]{4,0,3,2,1:T(8,128)(2,1)S(1)} collective-permute-done((bf16[64,3,1,1,128]{4,0,3,2,1:T(8,128)(2,1)S(1)}, bf16[64,3,1,1,128]{4,0,3,2,1:T(8,128)(2,1)S(1)}, u32[]{:S(2)}, u32[]{:S(2)}) %collective-permute-start.1) | collective-permute-done | bytes 49184 | tf_op jit(solution)/shard_map/ppermute | solution.py:26
  19.6 1.3 collective-permute-start.3
  20.9 3.1 %collective-permute-start.2 = (bf16[64,3,1,10,128]{4,0,3,2,1:T(8,128)(2,1)S(1)}, bf16[64,3,1,10,128]{4,0,3,2,1:T(8,128)(2,1)S(1)}, u32[]{:S(2)}, u32[]{:S(2)}) collective-permute-start(bf16[64,3,1,10,128]{4,0,3,2,1:T(8,128)(2,1)S(1)} %constant_dynamic-update-slice_fusion), channel_id=1, source_target_pairs={{0,1},{1,2},{2,3},{3,4},{4,5},{5,6},{6,7},{8,9},{9,10},{10,11},{11... | collective-permute-start | bytes 1474568 | tf_op jit(solution)/shard_map/ppermute | solution.py:25
  28.0 6.6 %collective-permute-start.4 = (f32[1024,256]{1,0:T(8,128)S(1)}, f32[1024,256]{1,0:T(8,128)S(1)}, u32[]{:S(2)}, u32[]{:S(2)}) collective-permute-start(f32[1024,256]{1,0:T(8,128)S(1)} %convolution_multiply_fusion), channel_id=1, source_target_pairs={{0,1},{1,0},{2,3},{3,2},{4,5},{5,4},{6,7},{7,6},{8,9},{9,8},{10,11... | collective-permute-start | bytes 3145736 | tf_op jit(solution)/shard_map/ppermute | solution.py:15
  34.6 2.3 collective-permute-done.4
  37.0 2.8 collective-permute-start.5
  39.9 23.7 %collective-permute-done.5 = f32[1024,256]{1,0:T(8,128)S(1)} collective-permute-done((f32[1024,256]{1,0:T(8,128)S(1)}, f32[1024,256]{1,0:T(8,128)S(1)}, u32[]{:S(2)}, u32[]{:S(2)}) %collective-permute-start.5) | collective-permute-done | bytes 1048608 | tf_op jit(solution)/shard_map/ppermute | solution.py:15
  63.7 3.7 %collective-permute-start.6 = (f32[1024,256]{1,0:T(8,128)S(1)}, f32[1024,256]{1,0:T(8,128)S(1)}, u32[]{:S(2)}, u32[]{:S(2)}) collective-permute-start(f32[1024,256]{1,0:T(8,128)S(1)} %add_select_fusion), channel_id=1, source_target_pairs={{0,4},{4,0},{1,5},{5,1},{2,6},{6,2},{3,7},{7,3},{8,12},{12,8},{9,1... | collective-permute-start | bytes 3145736 | tf_op jit(solution)/shard_map/ppermute | solution.py:15
  67.5 22.6 %collective-permute-done.6 = f32[1024,256]{1,0:T(8,128)S(1)} collective-permute-done((f32[1024,256]{1,0:T(8,128)S(1)}, f32[1024,256]{1,0:T(8,128)S(1)}, u32[]{:S(2)}, u32[]{:S(2)}) %collective-permute-start.6) | collective-permute-done | bytes 1048608 | tf_op jit(solution)/shard_map/ppermute | solution.py:15
  90.2 1.0 gather_fusion
  91.3 1.1 convolution_multiply_fusion.1
  92.7 53.0 %all-reduce.4.cloned.1.call-done = f32[256,256]{0,1:T(8,128)} async-done(((f32[256,256]{0,1:T(8,128)}), f32[256,256]{0,1:T(8,128)}) %all-reduce.4.cloned.1.call-update) | async-done | bytes 262160 | tf_op jit(solution)/shard_map/psum | solution.py:89
  145.7 1.1 copy.44
  146.8 1.0 fusion.20
  147.8 11.7 %cholesky.130 = f32[128,128]{1,0:T(8,128)S(1)} custom-call(f32[128,128]{1,0:T(8,128)S(1)} %cholesky.194), custom_call_target="Cholesky" | custom-call | tf_op jit(solution)/shard_map/jit(cholesky)/cholesky | solution.py:62
  159.6 9.8 %custom-call.14 = f32[1,128,128]{1,2,0:T(8,128)S(1)} custom-call(f32[1,128,128]{2,1,0:T(8,128)S(1)} %get-tuple-element.41), custom_call_target="InvertDiagBlocksLowerTriangular" | custom-call | tf_op jit(solution)/shard_map/jit(cholesky)/cholesky | solution.py:62
  169.9 11.7 %cholesky.147 = f32[128,128]{1,0:T(8,128)S(1)} custom-call(f32[128,128]{1,0:T(8,128)S(1)} %convolution_subtract_fusion.2), custom_call_target="Cholesky" | custom-call | tf_op jit(solution)/shard_map/jit(cholesky)/cholesky | solution.py:62
  184.4 27.4 %all-gather.3.cloned.1.call-done = f32[1024,256]{0,1:T(8,128)} async-done(((f32[256,256]{0,1:T(8,128)}), f32[1024,256]{0,1:T(8,128)}) %all-gather.3.cloned.1.call-update) | async-done | bytes 1048592 | tf_op jit(solution)/shard_map/all_gather | solution.py:90
  211.8 2.6 convolution_bitcast_fusion
  214.6 11.9 %cholesky.164 = f32[128,128]{1,0:T(8,128)S(1)} custom-call(f32[128,128]{1,0:T(8,128)S(1)} %cholesky.197), custom_call_target="Cholesky" | custom-call | tf_op jit(solution)/shard_map/jit(cholesky)/cholesky | solution.py:62
  226.6 9.8 %custom-call.15 = f32[1,128,128]{1,2,0:T(8,128)S(1)} custom-call(f32[1,128,128]{2,1,0:T(8,128)S(1)} %get-tuple-element.37), custom_call_target="InvertDiagBlocksLowerTriangular" | custom-call | tf_op jit(solution)/shard_map/jit(cholesky)/cholesky | solution.py:62
  236.8 11.7 %cholesky.181 = f32[128,128]{1,0:T(8,128)S(1)} custom-call(f32[128,128]{1,0:T(8,128)S(1)} %convolution_subtract_fusion.1), custom_call_target="Cholesky" | custom-call | tf_op jit(solution)/shard_map/jit(cholesky)/cholesky | solution.py:62
  251.3 4.2 %while.1 = (s32[]{:T(128)}, f32[256,256]{1,0:T(8,128)S(1)}, s32[2,2]{1,0:T(2,128)S(1)}, f32[2,128,128]{2,1,0:T(8,128)S(1)}, s32[]{:T(128)}) while((s32[]{:T(128)}, f32[256,256]{1,0:T(8,128)S(1)}, s32[2,2]{1,0:T(2,128)S(1)}, f32[2,128,128]{2,1,0:T(8,128)S(1)}, s32[]{:T(128)}) %tuple.38), condition=%wide.while_cond, body=%wide.while_body.sunk | while | flops 2 | bytes 131189 | solution.py:95
  252.1 1.4 bitcast_dynamic-update-slice_fusion.2
  254.1 1.4 bitcast_dynamic-update-slice_fusion.2
  255.5 19.7 %custom-call.12 = f32[2,128,128]{1,2,0:T(8,128)S(1)} custom-call(f32[2,128,128]{2,1,0:T(8,128)S(1)} %get-tuple-element.10), custom_call_target="InvertDiagBlocksLowerTriangular" | custom-call | tf_op jit(solution)/shard_map/jit(_solve_triangular)/triangular_solve | solution.py:95
  276.1 0.8 copy.48
  276.9 0.8 copy.49
  (64 shorter events, 11.5 us)
Async XLA Ops:
  7.2 138.5 %all-reduce.4.cloned.1.call-start = ((), (), s32[]{:S(2)}) async-start(), calls=%async_computation | async-start | bytes 524288 | tf_op jit(solution)/shard_map/psum | solution.py:89
  8.6 6.7 %collective-permute-start = (bf16[64,3,1,1,128]{4,0,3,2,1:T(8,128)(2,1)S(1)}, bf16[64,3,1,1,128]{4,0,3,2,1:T(8,128)(2,1)S(1)}, u32[]{:S(2)}, u32[]{:S(2)}) collective-permute-start(bf16[64,3,1,1,128]{4,0,3,2,1:T(8,128)(2,1)S(1)} %copy.62), channel_id=1, source_target_pairs={{0,8},{8,16},{16,24},{1,9},{9,17},{17,25},{2,10},{10,18},{18,26},{... | collective-permute-start | bytes 147464 | tf_op jit(solution)/shard_map/ppermute | solution.py:25
  13.6 6.0 %collective-permute-start.1 = (bf16[64,3,1,1,128]{4,0,3,2,1:T(8,128)(2,1)S(1)}, bf16[64,3,1,1,128]{4,0,3,2,1:T(8,128)(2,1)S(1)}, u32[]{:S(2)}, u32[]{:S(2)}) collective-permute-start(bf16[64,3,1,1,128]{4,0,3,2,1:T(8,128)(2,1)S(1)} %copy.63), channel_id=1, source_target_pairs={{8,0},{16,8},{24,16},{9,1},{17,9},{25,17},{10,2},{18,10},{26,18},{... | collective-permute-start | bytes 147464 | tf_op jit(solution)/shard_map/ppermute | solution.py:26
  19.6 5.1 %collective-permute-start.3 = (bf16[64,3,1,10,128]{4,0,3,2,1:T(8,128)(2,1)S(1)}, bf16[64,3,1,10,128]{4,0,3,2,1:T(8,128)(2,1)S(1)}, u32[]{:S(2)}, u32[]{:S(2)}) collective-permute-start(bf16[64,3,1,10,128]{4,0,3,2,1:T(8,128)(2,1)S(1)} %constant_dynamic-update-slice_fusion), channel_id=1, source_target_pairs={{1,0},{2,1},{3,2},{4,3},{5,4},{6,5},{7,6},{9,8},{10,9},{11,10},{12... | collective-permute-start | bytes 1474568 | tf_op jit(solution)/shard_map/ppermute | solution.py:26
  20.9 4.5 %collective-permute-start.2 = (bf16[64,3,1,10,128]{4,0,3,2,1:T(8,128)(2,1)S(1)}, bf16[64,3,1,10,128]{4,0,3,2,1:T(8,128)(2,1)S(1)}, u32[]{:S(2)}, u32[]{:S(2)}) collective-permute-start(bf16[64,3,1,10,128]{4,0,3,2,1:T(8,128)(2,1)S(1)} %constant_dynamic-update-slice_fusion), channel_id=1, source_target_pairs={{0,1},{1,2},{2,3},{3,4},{4,5},{5,6},{6,7},{8,9},{9,10},{10,11},{11... | collective-permute-start | bytes 1474568 | tf_op jit(solution)/shard_map/ppermute | solution.py:25
  26.0 1.0 copy-start
  26.5 1.0 copy-start.2
  28.0 8.9 %collective-permute-start.4 = (f32[1024,256]{1,0:T(8,128)S(1)}, f32[1024,256]{1,0:T(8,128)S(1)}, u32[]{:S(2)}, u32[]{:S(2)}) collective-permute-start(f32[1024,256]{1,0:T(8,128)S(1)} %convolution_multiply_fusion), channel_id=1, source_target_pairs={{0,1},{1,0},{2,3},{3,2},{4,5},{5,4},{6,7},{7,6},{8,9},{9,8},{10,11... | collective-permute-start | bytes 3145736 | tf_op jit(solution)/shard_map/ppermute | solution.py:15
  37.0 30.4 %copy-start.1 = (s32[1,1,256]{2,1,0:T(1,128)S(1)}, s32[1,1,256]{2,1,0:T(1,128)}, u32[]{:S(2)}) copy-start(s32[1,1,256]{2,1,0:T(1,128)} %param.10) | copy-start | bytes 3076
  37.0 26.5 %collective-permute-start.5 = (f32[1024,256]{1,0:T(8,128)S(1)}, f32[1024,256]{1,0:T(8,128)S(1)}, u32[]{:S(2)}, u32[]{:S(2)}) collective-permute-start(f32[1024,256]{1,0:T(8,128)S(1)} %add_select_fusion.1), channel_id=1, source_target_pairs={{0,2},{2,0},{1,3},{3,1},{4,6},{6,4},{5,7},{7,5},{8,10},{10,8},{9,1... | collective-permute-start | bytes 3145736 | tf_op jit(solution)/shard_map/ppermute | solution.py:15
  63.7 26.4 %collective-permute-start.6 = (f32[1024,256]{1,0:T(8,128)S(1)}, f32[1024,256]{1,0:T(8,128)S(1)}, u32[]{:S(2)}, u32[]{:S(2)}) collective-permute-start(f32[1024,256]{1,0:T(8,128)S(1)} %add_select_fusion), channel_id=1, source_target_pairs={{0,4},{4,0},{1,5},{5,1},{2,6},{6,2},{3,7},{7,3},{8,12},{12,8},{9,1... | collective-permute-start | bytes 3145736 | tf_op jit(solution)/shard_map/ppermute | solution.py:15
  92.5 119.3 %all-gather.3.cloned.1.call-start = ((), (), s32[]{:S(2)}) async-start(), calls=%async_computation.1 | async-start | bytes 1310720 | tf_op jit(solution)/shard_map/all_gather | solution.py:90
Sparse Core Ops, SparseCore 0:
  92.6 53.0 all-reduce.3
  184.4 27.2 all-gather.2
where the time goes:
time: 285 us
  waiting for transfers between devices  133 us (47%)
  other arithmetic  92.6 us (32%)
  starting transfers between devices  24 us (8%)
  between operations  17 us (6%)
  local copies, waits for them, and re-layouts  11.4 us (4%)
  matrix products  5.98 us (2%)
    another operation x13, other arithmetic, upper_factor(): return jnp.linalg.cholesky(gram_matrix).T  68.8 us
    psum x1, waiting for transfers between devices, on_device(): block_factor = upper_factor(lax.psum(local_gram, 'mix'))  53 us
    ppermute x3, waiting for transfers between devices, swapped(): return lax.ppermute(block, axis, route)  48.6 us
    all_gather x1, waiting for transfers between devices, on_device(): every_factor = lax.all_gather(block_factor[None], 'row', axis=0, tiled=True)  27.4 us
    another operation x2, other arithmetic, on_device(): solved = jax.scipy.linalg.solve_triangular(factor.T, picked.T, lower=True)  19.7 us
    ppermute x3, starting transfers between devices, swapped(): return lax.ppermute(block, axis, route)  13.2 us
    ppermute x2, starting transfers between devices, padded(): before = lax.ppermute(last, axis, up)  7.99 us
  transfers between devices with their start and end apart: 9, of which 8 were waited for; matrix products, arithmetic and copies ran while one was open for 1% of the time, Pallas kernels for 0%

commit v1 on v0

--- a/solution.py
+++ b/solution.py
@@ -3,6 +3,28 @@
 import jax.numpy as jnp
 from jax import lax
 from jax.sharding import PartitionSpec as P
+
+
+def laid_out(parts, dim):
+    shape = list(parts.shape[1:])
+    shape[dim] *= parts.shape[0]
+    return jnp.moveaxis(parts, 0, dim).reshape(shape)
+
+
+def gather_around(value, axis, dim):
+    size = lax.axis_size(axis)
+    pairs = [(i, (i + 1) % size) for i in range(size)]
+    back = [(b, a) for a, b in pairs]
+    lower, upper = ([], [])
+    for hop in range(size - 1):
+        if hop % 2 == 0:
+            lower.append(lax.ppermute(lower[-1] if lower else value, axis, pairs))
+        else:
+            upper.append(lax.ppermute(upper[-1] if upper else value, axis, back))
+    parts = jnp.stack([*lower[::-1], value, *upper])
+    shift = lax.axis_index(axis) - len(lower)
+    parts = parts[(jnp.arange(size) - shift) % size]
+    return laid_out(parts, dim)
 
 
 def swapped(block, axis, distance):
@@ -87,7 +109,7 @@
         / picked_total
     )
     block_factor = upper_factor(lax.psum(local_gram, "mix"))
-    every_factor = lax.all_gather(block_factor[None], "row", axis=0, tiled=True)
+    every_factor = gather_around(block_factor[None], "row", 0)
     stacked_gram = jnp.einsum(
         "bij,bil->jl", every_factor, every_factor, precision=lax.Precision.HIGHEST
     )

time: 285 us -> 276 us (0.968)
  waiting for transfers between devices: 133 us -> 122 us
  starting transfers between devices: 24 us -> 28.7 us
    all_gather x1 -> x0, waiting for transfers between devices: 27.4 us -> none  [on_device(): every_factor = lax.all_gather(block_factor[None], 'row', axis=0, tiled=True)]
    ppermute x0 -> x3, waiting for transfers between devices: none -> 15.5 us  [the longest x2 11.9 us: gather_around(): lower.append(lax.ppermute(lower[-1] if lower else value, axis, pairs))]
    ppermute x0 -> x3, starting transfers between devices: none -> 4.85 us  [the longest x2 2.46 us: gather_around(): lower.append(lax.ppermute(lower[-1] if lower else value, axis, pairs))]
  transfers between devices with their start and end apart: 9 -> 11, of which waited for: 8 -> 10; matrix products, arithmetic and copies ran while one was open for 1% -> 1% of each run, Pallas kernels for 0% -> 0%
where the time goes in v1:
time: 276 us
  waiting for transfers between devices  122 us (44%)
  other arithmetic  92.1 us (33%)
  starting transfers between devices  28.7 us (10%)
  between operations  16.9 us (6%)
  local copies, waits for them, and re-layouts  12 us (4%)
  matrix products  4.45 us (2%)
    another operation x13, other arithmetic, upper_factor(): return jnp.linalg.cholesky(gram_matrix).T  68.8 us
    psum x1, waiting for transfers between devices, on_device(): block_factor = upper_factor(lax.psum(local_gram, 'mix'))  53.2 us
    ppermute x3, waiting for transfers between devices, swapped(): return lax.ppermute(block, axis, route)  48.6 us
    another operation x2, other arithmetic, on_device(): solved = jax.scipy.linalg.solve_triangular(factor.T, picked.T, lower=True)  19.7 us
    ppermute x3, starting transfers between devices, swapped(): return lax.ppermute(block, axis, route)  13.2 us
    ppermute x2, waiting for transfers between devices, gather_around(): lower.append(lax.ppermute(lower[-1] if lower else value, axis, pairs))  11.9 us
    ppermute x2, starting transfers between devices, padded(): before = lax.ppermute(last, axis, up)  7.99 us
  transfers between devices with their start and end apart: 11, of which 10 were waited for; matrix products, arithmetic and copies ran while one was open for 1% of the time, Pallas kernels for 0%

profile of v1, /device:TPU:0, one launch (start us, length us, event | category | flops | bytes accessed | tf_op | source)
XLA Modules:
  0.0 275.9 jit_solution(6526038148077004636)
XLA Ops:
  7.2 1.4 fusion.48
  8.6 4.9 %collective-permute-start = (bf16[64,3,1,1,128]{4,0,3,2,1:T(8,128)(2,1)S(1)}, bf16[64,3,1,1,128]{4,0,3,2,1:T(8,128)(2,1)S(1)}, u32[]{:S(2)}, u32[]{:S(2)}) collective-permute-start(bf16[64,3,1,1,128]{4,0,3,2,1:T(8,128)(2,1)S(1)} %copy.55), channel_id=1, source_target_pairs={{0,8},{8,16},{16,24},{1,9},{9,17},{17,25},{2,10},{10,18},{18,26},{... | collective-permute-start | bytes 147464 | tf_op jit(solution)/shard_map/ppermute | solution.py:47
  13.5 1.3 collective-permute-start.1
  15.3 1.1 constant_dynamic-update-slice_fusion.1
  16.4 3.2 %collective-permute-done.1 = bf16[64,3,1,1,128]{4,0,3,2,1:T(8,128)(2,1)S(1)} collective-permute-done((bf16[64,3,1,1,128]{4,0,3,2,1:T(8,128)(2,1)S(1)}, bf16[64,3,1,1,128]{4,0,3,2,1:T(8,128)(2,1)S(1)}, u32[]{:S(2)}, u32[]{:S(2)}) %collective-permute-start.1) | collective-permute-done | bytes 49184 | tf_op jit(solution)/shard_map/ppermute | solution.py:48
  19.5 1.3 collective-permute-start.3
  20.8 3.1 %collective-permute-start.2 = (bf16[64,3,1,10,128]{4,0,3,2,1:T(8,128)(2,1)S(1)}, bf16[64,3,1,10,128]{4,0,3,2,1:T(8,128)(2,1)S(1)}, u32[]{:S(2)}, u32[]{:S(2)}) collective-permute-start(bf16[64,3,1,10,128]{4,0,3,2,1:T(8,128)(2,1)S(1)} %constant_dynamic-update-slice_fusion), channel_id=1, source_target_pairs={{0,1},{1,2},{2,3},{3,4},{4,5},{5,6},{6,7},{8,9},{9,10},{10,11},{11... | collective-permute-start | bytes 1474568 | tf_op jit(solution)/shard_map/ppermute | solution.py:47
  28.0 6.6 %collective-permute-start.4 = (f32[1024,256]{1,0:T(8,128)S(1)}, f32[1024,256]{1,0:T(8,128)S(1)}, u32[]{:S(2)}, u32[]{:S(2)}) collective-permute-start(f32[1024,256]{1,0:T(8,128)S(1)} %convolution_multiply_fusion), channel_id=1, source_target_pairs={{0,1},{1,0},{2,3},{3,2},{4,5},{5,4},{6,7},{7,6},{8,9},{9,8},{10,11... | collective-permute-start | bytes 3145736 | tf_op jit(solution)/shard_map/ppermute | solution.py:37
  34.6 2.3 collective-permute-done.4
  37.0 2.8 %collective-permute-start.5 = (f32[1024,256]{1,0:T(8,128)S(1)}, f32[1024,256]{1,0:T(8,128)S(1)}, u32[]{:S(2)}, u32[]{:S(2)}) collective-permute-start(f32[1024,256]{1,0:T(8,128)S(1)} %add_select_fusion.1), channel_id=1, source_target_pairs={{0,2},{2,0},{1,3},{3,1},{4,6},{6,4},{5,7},{7,5},{8,10},{10,8},{9,1... | collective-permute-start | bytes 3145736 | tf_op jit(solution)/shard_map/ppermute | solution.py:37
  39.9 23.7 %collective-permute-done.5 = f32[1024,256]{1,0:T(8,128)S(1)} collective-permute-done((f32[1024,256]{1,0:T(8,128)S(1)}, f32[1024,256]{1,0:T(8,128)S(1)}, u32[]{:S(2)}, u32[]{:S(2)}) %collective-permute-start.5) | collective-permute-done | bytes 1048608 | tf_op jit(solution)/shard_map/ppermute | solution.py:37
  63.7 3.7 %collective-permute-start.6 = (f32[1024,256]{1,0:T(8,128)S(1)}, f32[1024,256]{1,0:T(8,128)S(1)}, u32[]{:S(2)}, u32[]{:S(2)}) collective-permute-start(f32[1024,256]{1,0:T(8,128)S(1)} %add_select_fusion), channel_id=1, source_target_pairs={{0,4},{4,0},{1,5},{5,1},{2,6},{6,2},{3,7},{7,3},{8,12},{12,8},{9,1... | collective-permute-start | bytes 3145736 | tf_op jit(solution)/shard_map/ppermute | solution.py:37
  67.4 22.6 %collective-permute-done.6 = f32[1024,256]{1,0:T(8,128)S(1)} collective-permute-done((f32[1024,256]{1,0:T(8,128)S(1)}, f32[1024,256]{1,0:T(8,128)S(1)}, u32[]{:S(2)}, u32[]{:S(2)}) %collective-permute-start.6) | collective-permute-done | bytes 1048608 | tf_op jit(solution)/shard_map/ppermute | solution.py:37
  91.3 1.1 convolution_multiply_fusion.1
  92.5 53.2 %all-reduce.4.cloned.1.call-done = f32[256,256]{0,1:T(8,128)} async-done(((f32[256,256]{0,1:T(8,128)}), f32[256,256]{0,1:T(8,128)}) %all-reduce.4.cloned.1.call-update) | async-done | bytes 262160 | tf_op jit(solution)/shard_map/psum | solution.py:111
  145.7 1.1 copy.42
  147.8 11.7 %cholesky.130 = f32[128,128]{1,0:T(8,128)S(1)} custom-call(f32[128,128]{1,0:T(8,128)S(1)} %cholesky.194), custom_call_target="Cholesky" | custom-call | tf_op jit(solution)/shard_map/jit(cholesky)/cholesky | solution.py:84
  159.6 9.8 %custom-call.14 = f32[1,128,128]{1,2,0:T(8,128)S(1)} custom-call(f32[1,128,128]{2,1,0:T(8,128)S(1)} %get-tuple-element.43), custom_call_target="InvertDiagBlocksLowerTriangular" | custom-call | tf_op jit(solution)/shard_map/jit(cholesky)/cholesky | solution.py:84
  169.8 11.9 %cholesky.147 = f32[128,128]{1,0:T(8,128)S(1)} custom-call(f32[128,128]{1,0:T(8,128)S(1)} %convolution_subtract_fusion.2), custom_call_target="Cholesky" | custom-call | tf_op jit(solution)/shard_map/jit(cholesky)/cholesky | solution.py:84
  183.8 1.5 collective-permute-start.7
  185.4 2.4 collective-permute-start.9
  187.8 7.2 %collective-permute-done.7 = f32[1,256,256]{1,2,0:T(8,128)S(1)} collective-permute-done((f32[1,256,256]{1,2,0:T(8,128)S(1)}, f32[1,256,256]{1,2,0:T(8,128)S(1)}, u32[]{:S(2)}, u32[]{:S(2)}) %collective-permute-start.7) | collective-permute-done | bytes 262176 | tf_op jit(solution)/shard_map/ppermute | solution.py:21
  195.9 3.6 %collective-permute-done.9 = f32[1,256,256]{1,2,0:T(8,128)S(1)} collective-permute-done((f32[1,256,256]{1,2,0:T(8,128)S(1)}, f32[1,256,256]{1,2,0:T(8,128)S(1)}, u32[]{:S(2)}, u32[]{:S(2)}) %collective-permute-start.9) | collective-permute-done | bytes 262176 | tf_op jit(solution)/shard_map/ppermute | solution.py:23
  199.4 4.7 %collective-permute-done.8 = f32[1,256,256]{1,2,0:T(8,128)S(1)} collective-permute-done((f32[1,256,256]{1,2,0:T(8,128)S(1)}, f32[1,256,256]{1,2,0:T(8,128)S(1)}, u32[]{:S(2)}, u32[]{:S(2)}) %collective-permute-start.8) | collective-permute-done | bytes 262176 | tf_op jit(solution)/shard_map/ppermute | solution.py:21
  204.9 1.0 convolution_bitcast_fusion
  206.1 11.7 %cholesky.164 = f32[128,128]{1,0:T(8,128)S(1)} custom-call(f32[128,128]{1,0:T(8,128)S(1)} %cholesky.197), custom_call_target="Cholesky" | custom-call | tf_op jit(solution)/shard_map/jit(cholesky)/cholesky | solution.py:84
  217.9 9.8 %custom-call.15 = f32[1,128,128]{1,2,0:T(8,128)S(1)} custom-call(f32[1,128,128]{2,1,0:T(8,128)S(1)} %get-tuple-element.39), custom_call_target="InvertDiagBlocksLowerTriangular" | custom-call | tf_op jit(solution)/shard_map/jit(cholesky)/cholesky | solution.py:84
  228.2 11.7 %cholesky.181 = f32[128,128]{1,0:T(8,128)S(1)} custom-call(f32[128,128]{1,0:T(8,128)S(1)} %convolution_subtract_fusion.1), custom_call_target="Cholesky" | custom-call | tf_op jit(solution)/shard_map/jit(cholesky)/cholesky | solution.py:84
  242.7 4.1 %while.1 = (s32[]{:T(128)}, f32[256,256]{1,0:T(8,128)S(1)}, s32[2,2]{1,0:T(2,128)S(1)}, f32[2,128,128]{2,1,0:T(8,128)S(1)}, s32[]{:T(128)}) while((s32[]{:T(128)}, f32[256,256]{1,0:T(8,128)S(1)}, s32[2,2]{1,0:T(2,128)S(1)}, f32[2,128,128]{2,1,0:T(8,128)S(1)}, s32[]{:T(128)}) %tuple.39), condition=%wide.while_cond, body=%wide.while_body.sunk | while | flops 2 | bytes 131189 | solution.py:117
  243.4 1.4 bitcast_dynamic-update-slice_fusion.2
  245.4 1.4 bitcast_dynamic-update-slice_fusion.2
  246.8 19.7 %custom-call.12 = f32[2,128,128]{1,2,0:T(8,128)S(1)} custom-call(f32[2,128,128]{2,1,0:T(8,128)S(1)} %get-tuple-element.10), custom_call_target="InvertDiagBlocksLowerTriangular" | custom-call | tf_op jit(solution)/shard_map/jit(_solve_triangular)/triangular_solve | solution.py:117
  (71 shorter events, 15.9 us)
Async XLA Ops:
  7.2 138.5 %all-reduce.4.cloned.1.call-start = ((), (), s32[]{:S(2)}) async-start(), calls=%async_computation | async-start | bytes 524288 | tf_op jit(solution)/shard_map/psum | solution.py:111
  8.6 6.7 %collective-permute-start = (bf16[64,3,1,1,128]{4,0,3,2,1:T(8,128)(2,1)S(1)}, bf16[64,3,1,1,128]{4,0,3,2,1:T(8,128)(2,1)S(1)}, u32[]{:S(2)}, u32[]{:S(2)}) collective-permute-start(bf16[64,3,1,1,128]{4,0,3,2,1:T(8,128)(2,1)S(1)} %copy.55), channel_id=1, source_target_pairs={{0,8},{8,16},{16,24},{1,9},{9,17},{17,25},{2,10},{10,18},{18,26},{... | collective-permute-start | bytes 147464 | tf_op jit(solution)/shard_map/ppermute | solution.py:47
  13.5 6.0 %collective-permute-start.1 = (bf16[64,3,1,1,128]{4,0,3,2,1:T(8,128)(2,1)S(1)}, bf16[64,3,1,1,128]{4,0,3,2,1:T(8,128)(2,1)S(1)}, u32[]{:S(2)}, u32[]{:S(2)}) collective-permute-start(bf16[64,3,1,1,128]{4,0,3,2,1:T(8,128)(2,1)S(1)} %copy.56), channel_id=1, source_target_pairs={{8,0},{16,8},{24,16},{9,1},{17,9},{25,17},{10,2},{18,10},{26,18},{... | collective-permute-start | bytes 147464 | tf_op jit(solution)/shard_map/ppermute | solution.py:48
  19.5 5.1 %collective-permute-start.3 = (bf16[64,3,1,10,128]{4,0,3,2,1:T(8,128)(2,1)S(1)}, bf16[64,3,1,10,128]{4,0,3,2,1:T(8,128)(2,1)S(1)}, u32[]{:S(2)}, u32[]{:S(2)}) collective-permute-start(bf16[64,3,1,10,128]{4,0,3,2,1:T(8,128)(2,1)S(1)} %constant_dynamic-update-slice_fusion), channel_id=1, source_target_pairs={{1,0},{2,1},{3,2},{4,3},{5,4},{6,5},{7,6},{9,8},{10,9},{11,10},{12... | collective-permute-start | bytes 1474568 | tf_op jit(solution)/shard_map/ppermute | solution.py:48
  20.8 4.5 %collective-permute-start.2 = (bf16[64,3,1,10,128]{4,0,3,2,1:T(8,128)(2,1)S(1)}, bf16[64,3,1,10,128]{4,0,3,2,1:T(8,128)(2,1)S(1)}, u32[]{:S(2)}, u32[]{:S(2)}) collective-permute-start(bf16[64,3,1,10,128]{4,0,3,2,1:T(8,128)(2,1)S(1)} %constant_dynamic-update-slice_fusion), channel_id=1, source_target_pairs={{0,1},{1,2},{2,3},{3,4},{4,5},{5,6},{6,7},{8,9},{9,10},{10,11},{11... | collective-permute-start | bytes 1474568 | tf_op jit(solution)/shard_map/ppermute | solution.py:47
  25.9 1.0 copy-start
  26.4 1.0 copy-start.2
  28.0 8.9 %collective-permute-start.4 = (f32[1024,256]{1,0:T(8,128)S(1)}, f32[1024,256]{1,0:T(8,128)S(1)}, u32[]{:S(2)}, u32[]{:S(2)}) collective-permute-start(f32[1024,256]{1,0:T(8,128)S(1)} %convolution_multiply_fusion), channel_id=1, source_target_pairs={{0,1},{1,0},{2,3},{3,2},{4,5},{5,4},{6,7},{7,6},{8,9},{9,8},{10,11... | collective-permute-start | bytes 3145736 | tf_op jit(solution)/shard_map/ppermute | solution.py:37
  37.0 30.4 %copy-start.1 = (s32[1,1,256]{2,1,0:T(1,128)S(1)}, s32[1,1,256]{2,1,0:T(1,128)}, u32[]{:S(2)}) copy-start(s32[1,1,256]{2,1,0:T(1,128)} %param.10) | copy-start | bytes 3076
  37.0 26.5 %collective-permute-start.5 = (f32[1024,256]{1,0:T(8,128)S(1)}, f32[1024,256]{1,0:T(8,128)S(1)}, u32[]{:S(2)}, u32[]{:S(2)}) collective-permute-start(f32[1024,256]{1,0:T(8,128)S(1)} %add_select_fusion.1), channel_id=1, source_target_pairs={{0,2},{2,0},{1,3},{3,1},{4,6},{6,4},{5,7},{7,5},{8,10},{10,8},{9,1... | collective-permute-start | bytes 3145736 | tf_op jit(solution)/shard_map/ppermute | solution.py:37
  63.7 26.4 %collective-permute-start.6 = (f32[1024,256]{1,0:T(8,128)S(1)}, f32[1024,256]{1,0:T(8,128)S(1)}, u32[]{:S(2)}, u32[]{:S(2)}) collective-permute-start(f32[1024,256]{1,0:T(8,128)S(1)} %add_select_fusion), channel_id=1, source_target_pairs={{0,4},{4,0},{1,5},{5,1},{2,6},{6,2},{3,7},{7,3},{8,12},{12,8},{9,1... | collective-permute-start | bytes 3145736 | tf_op jit(solution)/shard_map/ppermute | solution.py:37
  183.8 11.1 %collective-permute-start.7 = (f32[1,256,256]{1,2,0:T(8,128)S(1)}, f32[1,256,256]{1,2,0:T(8,128)S(1)}, u32[]{:S(2)}, u32[]{:S(2)}) collective-permute-start(f32[1,256,256]{1,2,0:T(8,128)S(1)} %get-tuple-element.35), channel_id=1, source_target_pairs={{0,8},{8,16},{16,24},{24,0},{1,9},{9,17},{17,25},{25,1},{2,10},{10... | collective-permute-start | bytes 786440 | tf_op jit(solution)/shard_map/ppermute | solution.py:21
  185.4 14.1 %collective-permute-start.9 = (f32[1,256,256]{1,2,0:T(8,128)S(1)}, f32[1,256,256]{1,2,0:T(8,128)S(1)}, u32[]{:S(2)}, u32[]{:S(2)}) collective-permute-start(f32[1,256,256]{1,2,0:T(8,128)S(1)} %get-tuple-element.35), channel_id=1, source_target_pairs={{8,0},{16,8},{24,16},{0,24},{9,1},{17,9},{25,17},{1,25},{10,2},{18... | collective-permute-start | bytes 786440 | tf_op jit(solution)/shard_map/ppermute | solution.py:23
  194.9 9.2 %collective-permute-start.8 = (f32[1,256,256]{1,2,0:T(8,128)S(1)}, f32[1,256,256]{1,2,0:T(8,128)S(1)}, u32[]{:S(2)}, u32[]{:S(2)}) collective-permute-start(f32[1,256,256]{1,2,0:T(8,128)S(1)} %collective-permute-done.7), channel_id=1, source_target_pairs={{0,8},{8,16},{16,24},{24,0},{1,9},{9,17},{17,25},{25,1},{2,10},{10... | collective-permute-start | bytes 786440 | tf_op jit(solution)/shard_map/ppermute | solution.py:21
Sparse Core Ops, SparseCore 0:
  92.6 53.0 all-reduce.3
